TPU v7x, 128 devices: a whole 4x4x4 slice. The times are simulated.
128 devices in a mesh: shard: 32 (over y, x, core), tile: 4 (over z).
Axes of the slice: x: 4, y: 4, z: 4, core: 2. Of those that a mesh axis runs over, the one named last changes fastest.
Arguments:
- embeddings: float32 [131072, 768], P(('shard', 'tile')), may hold values from -12 to 12
- cluster_ids: int32 [131072], P(('shard', 'tile')), may hold values from 0 to 511, as said below
Outputs:
- soft_max_sim: float32 [131072], P(('shard', 'tile'))
Inputs may be any that keep to these rules, and one draw needn't show every extreme that they name: `cluster_ids`: cluster c is owned by group c // 16. Each device holds at most 64 rows of one group's clusters; in every draw, for each tile index, some group gets exactly 64 rows from every device of that tile index.
All inputs are finite; a program needn't handle non-finite values.
Results may differ from a plain program's by a relative error of at most 0.00053.
Values may be sent and summed in bfloat16 or wider, within the bound.
A program may use at most 64 MiB of HBM per device.

v0:
```python
import jax
import jax.numpy as jnp
from jax import lax
from jax.sharding import PartitionSpec as P

KG = 16


sharpness = 30.0
epsilon = 1e-06


def unit_rows(embeddings):
    energy = jnp.sum(embeddings * embeddings, axis=1, keepdims=True)
    return (embeddings * lax.rsqrt(energy + epsilon)).astype(jnp.bfloat16)


def pair_sums(left, left_labels, left_place, right, right_labels, right_place):
    count = left.shape[0]
    block = min(512, count)
    blocks = count // block

    def step(column_total, items):
        rows_block, labels_block, place_block = items
        scores = lax.dot_general(
            rows_block, right, (((1,), (1,)), ((), ())), preferred_element_type=jnp.float32
        )
        same = (labels_block[:, None] == right_labels[None, :]) & (labels_block[:, None] >= 0)
        same = same & (place_block[:, None] < right_place[None, :])
        terms = jnp.where(same, jnp.exp(sharpness * scores), 0.0)
        return (column_total + jnp.sum(terms, axis=0), jnp.sum(terms, axis=1))

    column_total, row_totals = lax.scan(
        step,
        jnp.zeros((right.shape[0],), jnp.float32),
        (
            left.reshape(blocks, block, left.shape[1]),
            left_labels.reshape(blocks, block),
            left_place.reshape(blocks, block),
        ),
    )
    return (row_totals.reshape(count), column_total)


def add_into(vector, start, values):
    current = lax.dynamic_slice_in_dim(vector, start, values.shape[0])
    return lax.dynamic_update_slice_in_dim(vector, current + values, start, 0)


def body(embeddings, cluster_ids):
    local_rows = embeddings.shape[0]
    shards = lax.axis_size("shard")
    tiles = lax.axis_size("tile")
    capacity = 2 * local_rows // shards
    slot_count = shards * capacity
    unit = unit_rows(embeddings)
    owner = cluster_ids // KG
    onehot = (owner[:, None] == jnp.arange(shards, dtype=jnp.int32)[None, :]).astype(jnp.int32)
    ranks = jnp.sum((jnp.cumsum(onehot, axis=0) - 1) * onehot, axis=1)
    slots = owner * capacity + ranks
    outgoing = jnp.zeros((slot_count, unit.shape[1]), jnp.bfloat16).at[slots].set(unit)
    outgoing_labels = jnp.full((slot_count,), -1, jnp.int32).at[slots].set(cluster_ids)
    arrived, arrived_labels = (
        lax.all_to_all(
            outgoing.reshape(shards, capacity, unit.shape[1]),
            "shard",
            split_axis=0,
            concat_axis=0,
            tiled=True,
        ),
        lax.all_to_all(
            outgoing_labels.reshape(shards, capacity),
            "shard",
            split_axis=0,
            concat_axis=0,
            tiled=True,
        ),
    )
    owned = arrived.reshape(slot_count, unit.shape[1])
    owned_labels = arrived_labels.reshape(slot_count)
    tile_index = lax.axis_index("tile")
    own_start = tile_index * slot_count
    own_place = own_start + jnp.arange(slot_count, dtype=jnp.int32)
    group_size = tiles * slot_count
    initial = (jnp.zeros((slot_count,), jnp.float32), jnp.zeros((group_size,), jnp.float32))
    start = jnp.int32(0)
    piece_rows = lax.all_gather(owned, "tile", axis=0, tiled=True)
    piece_labels = lax.all_gather(owned_labels, "tile", axis=0, tiled=True)
    width = piece_rows.shape[0]
    piece_place = jnp.arange(width, dtype=jnp.int32)

    def work(state):
        row_part, column_part = pair_sums(
            owned, owned_labels, own_place, piece_rows, piece_labels, piece_place
        )
        return (row_part, add_into(state[1], start, column_part))

    def skip(state):
        return state

    row_sum, column_sum = lax.cond(start + width > own_start, work, skip, initial)
    group_total = add_into(column_sum, own_start, row_sum)
    own_totals = lax.psum_scatter(
        group_total.astype(jnp.bfloat16), "tile", scatter_dimension=0, tiled=True
    ).astype(jnp.float32)
    returned = lax.all_to_all(
        own_totals.reshape(shards, capacity), "shard", split_axis=0, concat_axis=0, tiled=True
    )
    totals = returned.reshape(slot_count)[slots]
    return jnp.log(1.0 + totals)


def solution(mesh):
    in_specs = (P(("shard", "tile"), None), P(("shard", "tile")))
    out_specs = P(("shard", "tile"))
    return jax.shard_map(body, mesh=mesh, in_specs=in_specs, out_specs=out_specs, check_vma=False)
```

profile of v0, /device:TPU:1, one launch (start us, length us, event | category | flops | bytes accessed | tf_op | source)
XLA Modules:
  0.0 298.9 jit_solution(13858667314509937433)
XLA Ops:
  6.5 0.0 copy-start
  6.5 0.0 all-gather.2.cloned.1.call-start
  6.5 0.8 add_select_fusion
  7.4 9.0 %reduce-window.6 = s32[32,8,128]{2,1,0:T(8,128)S(1)} reduce-window(s32[32,8,128]{2,1,0:T(8,128)S(1)} %fusion.8, s32[]{:T(128)} %constant.42.clone.1), window={size=1x1x128 pad=0_0x0_0x127_0}, to_apply=%region_0.0 | reduce-window | flops 4161536 | bytes 262148 | tf_op jit(solution)/shard_map/reduce-window
  16.4 0.1 slice.10
  16.5 0.1 copy.5
  16.7 0.1 copy.6
  16.8 0.1 add_add_fusion
  16.9 0.7 broadcast_clamp_fusion
  17.6 2.2 multiply_reduce_fusion
  19.8 0.0 copy-done
  19.8 7.7 %scatter_custom_fusion = bf16[2048,768]{1,0:T(8,128)(2,1)} fusion(s32[1024]{0:T(1024)S(1)} %get-tuple-element.139, f32[1024,768]{1,0:T(8,128)S(1)} %copy-done, f32[1024]{0:T(1024)S(1)} %add_rsqrt_fusion, bf16[]{:T(256)} %constant.34.clone.1), kind=kCustom, calls=%fused_computation.14 | custom fusion | flops 1572864 | bytes 6295554 | tf_op jit(solution)/shard_map/scatter | solution.py:61
  27.5 48.2 %all_to_all.28 = bf16[32,64,768]{2,1,0:T(8,128)(2,1)} all-to-all(bf16[32,64,768]{2,1,0:T(8,128)(2,1)} %bitcast.46), channel_id=1, replica_groups=mesh['shard'=32,'tile'=4] {'shard'}, dimensions={0} | all-to-all | bytes 6291456 | tf_op jit(solution)/shard_map/all_to_all | solution.py:64
  75.7 0.0 copy-start.1
  75.7 0.0 all-gather.2.cloned.1.call-update
  75.8 4.5 %scatter_custom_fusion.1 = s32[2048]{0:T(1024)S(1)} fusion(s32[1024]{0:T(1024)S(1)} %get-tuple-element.139, s32[1024]{0:T(1024)} %param.7, s32[]{:T(128)} %constant.64.clone.1), kind=kCustom, calls=%fused_computation.33 | custom fusion | bytes 8704 | tf_op jit(solution)/shard_map/scatter | solution.py:62
  80.2 0.7 all_to_all.18
  80.9 3.9 %all-to-all-start.1 = ((s32[32,1,64]{2,1,0:T(1,128)}), s32[32,1,64]{2,1,0:T(1,128)S(1)}, u32[]{:S(2)}, u32[]{:S(2)}) async-start(s32[32,1,64]{2,1,0:T(1,128)} %all_to_all.18), calls=%async_computation.1 | async-start | bytes 32768 | tf_op jit(solution)/shard_map/all_to_all | solution.py:71
  84.8 0.0 copy-done.1
  84.8 0.7 dynamic-slice
  86.1 5.8 %all-to-all-done.1 = s32[32,1,64]{2,1,0:T(1,128)S(1)} async-done(((s32[32,1,64]{2,1,0:T(1,128)}), s32[32,1,64]{2,1,0:T(1,128)S(1)}, u32[]{:S(2)}, u32[]{:S(2)}) %all-to-all-start.1) | async-done | bytes 8224 | tf_op jit(solution)/shard_map/all_to_all | solution.py:71
  91.9 0.5 broadcast.103
  92.4 0.7 reduce.6
  93.1 0.1 reshape.70
  93.2 11.8 %all_gather.6 = s32[8192]{0:T(1024)S(1)} all-gather(s32[2048]{0:T(1024)S(1)} %reshape.70), channel_id=1, replica_groups=mesh['shard'=32,'tile'=4] {'tile'}, dimensions={0}, use_global_device_ids=true | all-gather | bytes 40960 | tf_op jit(solution)/shard_map/all_gather | solution.py:88
  104.9 88.2 %all-gather.2.cloned.1.call-done = bf16[8192,768]{1,0:T(8,128)(2,1)} async-done(((bf16[2048,768]{1,0:T(8,128)(2,1)}), bf16[8192,768]{1,0:T(8,128)(2,1)}) %all-gather.2.cloned.1.call-update) | async-done | bytes 12582928 | tf_op jit(solution)/shard_map/all_gather | solution.py:87
  193.1 58.5 %conditional.1 = (f32[2048]{0:T(1024)S(1)}, f32[8192]{0:T(1024)}) conditional(s32[]{:T(128)} %convert_element_type.15, () %tuple.17, (bf16[32,64,768]{2,1,0:T(8,128)(2,1)}, s32[32,1,64]{2,1,0:T(1,128)S(1)}, s32[]{:T(128)}, s32[2048]{0:T(1024)S(1)}, s32[8192]{0:T(1024)S(1)}, /*index=5*/s32[8192]{0:T(1024)S(1)}, bf16[8192,768]{1,0:T(8,128)(2,1)}) %tuple.18), branch_computations={%region_6.7_spmd, %region_7.12_spmd} | conditional | flops 6476015616 | bytes 13653747 | solution.py:101
  193.1 0.1 reshape_reshape.4
  193.2 58.3 %while.12 = (s32[]{:T(128)}, f32[8192]{0:T(1024)}, f32[4,512]{1,0:T(4,128)S(1)}, s32[4,512]{1,0:T(4,128)S(1)}, s32[8192]{0:T(1024)S(1)}, /*index=5*/s32[4,512]{1...) while((s32[]{:T(128)}, f32[8192]{0:T(1024)}, ...), condition=%wide.region_11.11_spmd.clone, body=%wide.region_8.10_spmd.clone.sunk | while | flops 6476013568 | bytes 13588095 | solution.py:33
  193.2 13.3 %fusion.19 = (f32[512]{0:T(512)S(1)}, f32[8192]{0:T(1024)S(1)}) fusion(bf16[8192,768]{1,0:T(8,128)(2,1)} %get-tuple-element.237, bf16[4,512,768]{2,1,0:T(8,128)(2,1)} %get-tuple-element.236, s32[]{:T(128)} %get-tuple-element.218, s32[8192]{0:T(1024)S(1)} %get-tuple-element.235, s32[512]{0:T(512)S(1)} %bitcast.51, ...), kind=kOutput, calls=%fused_computation.40.clone.1 | convolution fusion | flops 6475996672 | bytes 13474816 | tf_op jit(solution)/shard_map/cond/branch_1_fun/while/body/eval_jaxpr/dot_general | solution.py:25
  206.6 0.6 select_add_fusion.2
  207.3 13.3 %fusion.19 = (f32[512]{0:T(512)S(1)}, f32[8192]{0:T(1024)S(1)}) fusion(bf16[8192,768]{1,0:T(8,128)(2,1)} %get-tuple-element.237, bf16[4,512,768]{2,1,0:T(8,128)(2,1)} %get-tuple-element.236, s32[]{:T(128)} %get-tuple-element.218, s32[8192]{0:T(1024)S(1)} %get-tuple-element.235, s32[512]{0:T(512)S(1)} %bitcast.51, ...), kind=kOutput, calls=%fused_computation.40.clone.1 | convolution fusion | flops 6475996672 | bytes 13474816 | tf_op jit(solution)/shard_map/cond/branch_1_fun/while/body/eval_jaxpr/dot_general | solution.py:25
  220.6 1.4 select_add_fusion.2
  222.0 13.3 %fusion.19 = (f32[512]{0:T(512)S(1)}, f32[8192]{0:T(1024)S(1)}) fusion(bf16[8192,768]{1,0:T(8,128)(2,1)} %get-tuple-element.237, bf16[4,512,768]{2,1,0:T(8,128)(2,1)} %get-tuple-element.236, s32[]{:T(128)} %get-tuple-element.218, s32[8192]{0:T(1024)S(1)} %get-tuple-element.235, s32[512]{0:T(512)S(1)} %bitcast.51, ...), kind=kOutput, calls=%fused_computation.40.clone.1 | convolution fusion | flops 6475996672 | bytes 13474816 | tf_op jit(solution)/shard_map/cond/branch_1_fun/while/body/eval_jaxpr/dot_general | solution.py:25
  235.4 1.4 select_add_fusion.2
  236.8 13.3 %fusion.19 = (f32[512]{0:T(512)S(1)}, f32[8192]{0:T(1024)S(1)}) fusion(bf16[8192,768]{1,0:T(8,128)(2,1)} %get-tuple-element.237, bf16[4,512,768]{2,1,0:T(8,128)(2,1)} %get-tuple-element.236, s32[]{:T(128)} %get-tuple-element.218, s32[8192]{0:T(1024)S(1)} %get-tuple-element.235, s32[512]{0:T(512)S(1)} %bitcast.51, ...), kind=kOutput, calls=%fused_computation.40.clone.1 | convolution fusion | flops 6475996672 | bytes 13474816 | tf_op jit(solution)/shard_map/cond/branch_1_fun/while/body/eval_jaxpr/dot_general | solution.py:25
  250.2 1.4 select_add_fusion.2
  251.6 1.3 add_dynamic-update-slice_fusion
  252.9 0.8 convert_element_type.18
  253.6 12.0 %all-reduce = bf16[8192]{0:T(1024)(128)(2,1)S(1)} all-reduce(bf16[8192]{0:T(1024)(128)(2,1)S(1)} %convert_element_type.18), channel_id=2, replica_groups=mesh['shard'=32,'tile'=4] {'tile'}, use_global_device_ids=true, to_apply=%region_12.13.clone | all-reduce | flops 8192 | bytes 32768
  265.6 0.1 reshape.73
  265.7 18.3 %all_to_all.29 = f32[32,1,64]{2,1,0:T(1,128)S(1)} all-to-all(f32[32,1,64]{2,1,0:T(1,128)S(1)} %reshape.73), channel_id=1, replica_groups=mesh['shard'=32,'tile'=4] {'shard'}, dimensions={0} | all-to-all | bytes 16384 | tf_op jit(solution)/shard_map/all_to_all | solution.py:106
  284.0 0.5 broadcast.104
  284.5 0.7 reduce.7
  285.2 0.1 reshape.72
  285.3 6.1 %gather_fusion = f32[1024]{0:T(1024)S(1)} fusion(f32[2048]{0:T(1024)S(1)} %reshape.72, s32[1024]{0:T(1024)S(1)} %get-tuple-element.138), kind=kCustom, calls=%fused_computation | custom fusion | bytes 12288 | tf_op jit(solution)/shard_map/gather | solution.py:109
  291.4 0.6 add_log_fusion
  (25 shorter events, 0.3 us)
Async XLA Ops:
  6.5 13.3 %copy-start = (f32[1024,768]{1,0:T(8,128)S(1)}, f32[1024,768]{1,0:T(8,128)}, u32[]{:S(2)}) copy-start(f32[1024,768]{1,0:T(8,128)} %param.6) | copy-start | bytes 9437188
  6.5 186.6 %all-gather.2.cloned.1.call-start = ((), (), s32[]{:S(2)}) async-start(), calls=%async_computation.3 | async-start | bytes 15728640 | tf_op jit(solution)/shard_map/all_gather | solution.py:87
  75.7 9.1 %copy-start.1 = (u32[128]{0:T(128)S(1)}, u32[128]{0:T(128)}, u32[]{:S(2)}) copy-start(u32[128]{0:T(128)} %constant.71) | copy-start | bytes 1540
  80.9 10.9 %all-to-all-start.1 = ((s32[32,1,64]{2,1,0:T(1,128)}), s32[32,1,64]{2,1,0:T(1,128)S(1)}, u32[]{:S(2)}, u32[]{:S(2)}) async-start(s32[32,1,64]{2,1,0:T(1,128)} %all_to_all.18), calls=%async_computation.1 | async-start | bytes 32768 | tf_op jit(solution)/shard_map/all_to_all | solution.py:71
Sparse Core Ops, SparseCore 0:
  75.9 117.1 all-gather.1
where the time goes:
time: 300 us; the launch traced here: 299 us
  waiting for transfers between devices  93.9 us (31%)
  blocking collectives  90.2 us (30%)
  matrix products  53.3 us (18%)
  other arithmetic  29.4 us (10%)
  between operations  14.2 us (5%)
  local copies, waits for them, and re-layouts  13.8 us (5%)
  starting transfers between devices  3.85 us (1%)
    all_gather x1, waiting for transfers between devices, body(): piece_rows = lax.all_gather(owned, 'tile', axis=0, tiled=True)  88.2 us
    dot_general x4, matrix products, step(): lax.dot_general(rows_block, right, (((1,), (1,)), ((), ())), preferred_el...  53.3 us
    all_to_all x1, blocking collectives, body(): lax.all_to_all(outgoing.reshape(shards, capacity, unit.shape[1]), 'shard'...  48.2 us
    all_to_all x1, blocking collectives, body(): lax.all_to_all(own_totals.reshape(shards, capacity), 'shard', split_axis=...  18.3 us
    unnamed x1, blocking collectives  12 us
    all_gather x1, blocking collectives, body(): piece_labels = lax.all_gather(owned_labels, 'tile', axis=0, tiled=True)  11.8 us
    another operation x3, other arithmetic  9.05 us
    scatter x1, other arithmetic, body(): jnp.zeros((slot_count, unit.shape[1]), jnp.bfloat16).at[slots].set(unit)  7.72 us
  transfers between devices with their start and end apart: 2, of which 2 were waited for; matrix products, arithmetic and copies ran while one was open for 2% of the time, Pallas kernels for 0%

commit v1 on v0

v1 whole, which is shorter than its diff:
```python
import functools
import math

import jax
import jax.numpy as jnp
from jax import lax
from jax.experimental import pallas as pl
from jax.experimental.pallas import tpu as pltpu
from jax.sharding import PartitionSpec as P

KG = 16
SHARDS = 32
CAP = 64
SLOTS = SHARDS * CAP
LANES = 128
MESH = pl.DeviceIdType.MESH

sharpness = 30.0
epsilon = 1e-06
EXP2_SCALE = sharpness / math.log(2.0)
ROW_BLOCK = 512


def unit_rows(embeddings):
    energy = jnp.sum(embeddings * embeddings, axis=1, keepdims=True)
    return (embeddings * lax.rsqrt(energy + epsilon)).astype(jnp.bfloat16)


def kernel(
    rows_ref, labels_ref, out_ref,
    rows, labels, row_labels, row_acc, col_f, col_h, col_in, totals, returned,
    local_sem, a2a_send, a2a_recv, lab_send, lab_recv, z_send, z_recv,
    zlab_send, zlab_recv, col_send, col_recv, ret_send, ret_recv,
):
    s = lax.axis_index("shard")
    t = lax.axis_index("tile")
    core = s % 2
    x = (s // 2) % 4
    y = s // 8
    up = (t + 1) % 4
    down = (t + 3) % 4
    high = t // 2
    f_device = (t + 2) * (1 - high) + (3 - t) * high
    h_device = t + 1 - 2 * (t % 2)
    f_slot = 2 - t % 2
    h_slot = 1 + t % 2

    def chip_at(step, sign):
        q = (step * 5) % 16
        return ((y + sign * (q // 4) + 4) % 4) * 4 + (x + sign * (q % 4) + 4) % 4

    def peer(i, sign):
        return chip_at(i // 2, sign) * 2 + (core + i % 2) % 2

    def chunk(slot, p):
        return rows.at[slot, pl.ds(pl.multiple_of(p * CAP, CAP), CAP)]

    barrier = pltpu.get_barrier_semaphore()

    @pl.loop(1, SHARDS)
    def _(i):
        pl.semaphore_signal(barrier, inc=1, device_id=(peer(i, 1), t), device_id_type=MESH)

    @pl.loop(1, 4)
    def _(i):
        pl.semaphore_signal(barrier, inc=1, device_id=(s, (t + i) % 4), device_id_type=MESH)

    own_rows = pltpu.make_async_copy(rows_ref.at[s], chunk(0, s), local_sem.at[0])
    own_labels = pltpu.make_async_copy(labels_ref.at[s], labels.at[0, s], local_sem.at[1])
    own_rows.start()
    own_labels.start()
    pl.semaphore_wait(barrier, SHARDS - 1 + 3)

    def label_copy(i):
        p = peer(i, 1)
        return pltpu.make_async_remote_copy(
            src_ref=labels_ref.at[p], dst_ref=labels.at[0, s],
            send_sem=lab_send.at[i], recv_sem=lab_recv.at[i],
            device_id=(p, t), device_id_type=MESH,
        )

    def label_arrival(i):
        p = peer(i, -1)
        return pltpu.make_async_remote_copy(
            src_ref=labels_ref.at[p], dst_ref=labels.at[0, p],
            send_sem=lab_send.at[i], recv_sem=lab_recv.at[i],
            device_id=(p, t), device_id_type=MESH,
        )

    def row_copy(i):
        p = peer(i, 1)
        return pltpu.make_async_remote_copy(
            src_ref=rows_ref.at[p], dst_ref=chunk(0, s),
            send_sem=a2a_send.at[i], recv_sem=a2a_recv.at[i],
            device_id=(p, t), device_id_type=MESH,
        )

    def row_arrival(i):
        p = peer(i, -1)
        return pltpu.make_async_remote_copy(
            src_ref=rows_ref.at[p], dst_ref=chunk(0, p),
            send_sem=a2a_send.at[i], recv_sem=a2a_recv.at[i],
            device_id=(p, t), device_id_type=MESH,
        )

    def z_copy(source, target, device, i):
        p = peer(i, -1)
        return pltpu.make_async_remote_copy(
            src_ref=chunk(source, p), dst_ref=chunk(target, p),
            send_sem=z_send.at[target - 1, i], recv_sem=z_recv.at[target - 1, i],
            device_id=(s, device), device_id_type=MESH,
        )

    def zlab_copy(source, target, device):
        return pltpu.make_async_remote_copy(
            src_ref=labels.at[source], dst_ref=labels.at[target],
            send_sem=zlab_send.at[target - 1], recv_sem=zlab_recv.at[target - 1],
            device_id=(s, device), device_id_type=MESH,
        )

    @pl.loop(1, SHARDS)
    def _(i):
        label_copy(i).start()

    @pl.loop(1, SHARDS)
    def _(i):
        row_copy(i).start()

    def send_own(i):
        @pl.when(t != 3)
        def _():
            z_copy(0, 2, up, i).start()

        @pl.when(t != 2)
        def _():
            z_copy(0, 1, down, i).start()

    def relay(i):
        @pl.when(t == 3)
        def _():
            z_copy(0, 2, up, i).wait_recv()
            z_copy(2, 2, up, i).start()

        @pl.when(t == 2)
        def _():
            z_copy(0, 1, down, i).wait_recv()
            z_copy(1, 1, down, i).start()

    own_rows.wait()
    own_labels.wait()
    send_own(0)

    def forward(i):
        row_arrival(i).wait_recv()
        send_own(i)

        @pl.when(i % 2 == 1)
        def _():
            relay(i // 2)

    @pl.loop(1, 6)
    def _(i):
        forward(i)

    @pl.loop(1, SHARDS)
    def _(i):
        label_arrival(i).wait_recv()

    @pl.when(t != 3)
    def _():
        zlab_copy(0, 2, up).start()

    @pl.when(t != 2)
    def _():
        zlab_copy(0, 1, down).start()

    def pair_labels(slot, c):
        return labels[slot, 2 * c] + labels[slot, 2 * c + 1]

    @pl.loop(0, SLOTS // LANES)
    def _(c):
        wide = jnp.broadcast_to(pair_labels(0, c), (LANES, LANES))
        row_labels[pl.ds(pl.multiple_of(c * LANES, LANES), LANES), :] = wide.astype(jnp.float32).T
        row_acc[pl.ds(pl.multiple_of(c * LANES, LANES), LANES), :] = jnp.zeros((LANES, LANES), jnp.float32)

    @pl.loop(6, SHARDS)
    def _(i):
        forward(i)

    zlab_copy(0, 2, up).wait_recv()
    zlab_copy(0, 1, down).wait_recv()

    @pl.when(t == 3)
    def _():
        zlab_copy(2, 2, up).start()

    @pl.when(t == 2)
    def _():
        zlab_copy(1, 1, down).start()

    def square(slot, chips, row_start, row_blocks, col_ref):
        columns = jnp.concatenate(
            [rows[slot, pl.ds(pl.multiple_of(c * LANES, LANES), LANES), :] for c in chips], axis=0
        )
        column_labels = [
            jnp.broadcast_to(pair_labels(slot, c), (8, LANES)).astype(jnp.float32)[0:1] for c in chips
        ]

        def block(m, sums):
            start = pl.multiple_of(row_start + m * ROW_BLOCK, ROW_BLOCK)
            here = pl.ds(start, ROW_BLOCK)
            scores = lax.dot_general(
                rows[0, here, :], columns, (((1,), (1,)), ((), ())),
                preferred_element_type=jnp.float32,
            )
            left = row_labels[here, :]
            added = None
            new_sums = []
            for n, c in enumerate(chips):
                same = left == column_labels[n]
                if col_ref is None:
                    down_index = lax.broadcasted_iota(jnp.int32, (ROW_BLOCK, LANES), 0)
                    along = lax.broadcasted_iota(jnp.int32, (ROW_BLOCK, LANES), 1)
                    same = same & ((down_index - along) != (c * LANES - start))
                terms = jnp.where(
                    same, jnp.exp2(scores[:, n * LANES:(n + 1) * LANES] * EXP2_SCALE), 0.0
                )
                added = terms if added is None else added + terms
                if col_ref is not None:
                    new_sums.append(sums[n] + jnp.sum(terms, axis=0, keepdims=True))
            row_acc[here, :] += added
            return tuple(new_sums)

        zero = tuple(jnp.zeros((1, LANES), jnp.float32) for _ in chips) if col_ref is not None else ()
        sums = lax.fori_loop(0, row_blocks, block, zero)
        if col_ref is not None:
            for n, c in enumerate(chips):
                col_ref[c] = sums[n]

    @pl.loop(0, 8)
    def _(j):
        @pl.loop(0, 2)
        def _(k):
            relay(16 + 2 * j + k)

        chips = [chip_at(2 * j, -1), chip_at(2 * j + 1, -1)]
        square(0, chips, 0, SLOTS // ROW_BLOCK, None)

        @pl.loop(0, 4)
        def _(k):
            z_copy(0, f_slot, up, 4 * j + k).wait_recv()

            @pl.when(t < 2)
            def _():
                z_copy(0, h_slot, up, 4 * j + k).wait_recv()

        square(f_slot, chips, 0, SLOTS // ROW_BLOCK, col_f)
        for n in range(2):
            half = (chips[n] // 8 + t) % 2
            square(h_slot, [chips[n]], half * (SLOTS // 2), SLOTS // 2 // ROW_BLOCK, col_h)

    def col_copy(source, k, device):
        return pltpu.make_async_remote_copy(
            src_ref=source, dst_ref=col_in.at[k],
            send_sem=col_send.at[k], recv_sem=col_recv.at[k],
            device_id=(s, device), device_id_type=MESH,
        )

    copy_f = col_copy(col_f, 0, f_device)
    copy_h = col_copy(col_h, 1, h_device)
    copy_f.start()
    copy_h.start()

    @pl.loop(0, SLOTS // LANES)
    def _(c):
        part = row_acc[pl.ds(pl.multiple_of(c * LANES, LANES), LANES), :]
        totals[c] = jnp.sum(part.T, axis=0, keepdims=True)

    copy_f.wait_recv()
    copy_h.wait_recv()

    @pl.loop(0, SLOTS // LANES)
    def _(c):
        totals[c] = totals[c] + col_in[0, c] + col_in[1, c]

    def ret_copy(i, p, place):
        return pltpu.make_async_remote_copy(
            src_ref=totals.at[p // 2], dst_ref=returned.at[place],
            send_sem=ret_send.at[i], recv_sem=ret_recv.at[i],
            device_id=(p, t), device_id_type=MESH,
        )

    @pl.loop(1, SHARDS)
    def _(i):
        ret_copy(i, peer(i, 1), s).start()

    returned[s] = totals[s // 2]

    @pl.loop(1, SHARDS)
    def _(i):
        label_copy(i).wait_send()
        row_copy(i).wait_send()

    @pl.loop(0, SHARDS)
    def _(i):
        z_copy(0, 1, down, i).wait_send()
        z_copy(0, 2, up, i).wait_send()

    zlab_copy(0, 1, down).wait_send()
    zlab_copy(0, 2, up).wait_send()
    copy_f.wait_send()
    copy_h.wait_send()

    @pl.loop(1, SHARDS)
    def _(i):
        p = peer(i, -1)
        ret_copy(i, p, p).wait_recv()
        ret_copy(i, peer(i, 1), s).wait_send()

    out_ref[...] = returned[...]


def exchange(outgoing, outgoing_labels):
    width = outgoing.shape[-1]
    dma = pltpu.SemaphoreType.DMA
    return pl.pallas_call(
        kernel,
        out_shape=jax.ShapeDtypeStruct((SHARDS, 1, LANES), jnp.float32),
        in_specs=[pl.BlockSpec(memory_space=pl.ANY), pl.BlockSpec(memory_space=pltpu.VMEM)],
        out_specs=pl.BlockSpec(memory_space=pltpu.VMEM),
        scratch_shapes=[
            pltpu.VMEM((3, SLOTS, width), jnp.bfloat16),
            pltpu.VMEM((3, SHARDS, 1, LANES), jnp.int32),
            pltpu.VMEM((SLOTS, LANES), jnp.float32),
            pltpu.VMEM((SLOTS, LANES), jnp.float32),
            pltpu.VMEM((SLOTS // LANES, 1, LANES), jnp.float32),
            pltpu.VMEM((SLOTS // LANES, 1, LANES), jnp.float32),
            pltpu.VMEM((2, SLOTS // LANES, 1, LANES), jnp.float32),
            pltpu.VMEM((SLOTS // LANES, 1, LANES), jnp.float32),
            pltpu.VMEM((SHARDS, 1, LANES), jnp.float32),
            dma((2,)), dma((SHARDS,)), dma((SHARDS,)), dma((SHARDS,)), dma((SHARDS,)),
            dma((2, SHARDS)), dma((2, SHARDS)), dma((2,)), dma((2,)), dma((2,)), dma((2,)),
            dma((SHARDS,)), dma((SHARDS,)),
        ],
        compiler_params=pltpu.CompilerParams(collective_id=0, has_side_effects=True),
    )(outgoing, outgoing_labels)


def body(embeddings, cluster_ids):
    unit = unit_rows(embeddings)
    owner = cluster_ids // KG
    onehot = (owner[:, None] == jnp.arange(SHARDS, dtype=jnp.int32)[None, :]).astype(jnp.int32)
    ranks = jnp.sum((jnp.cumsum(onehot, axis=0) - 1) * onehot, axis=1)
    slots = owner * CAP + ranks
    outgoing = jnp.zeros((SLOTS, unit.shape[1]), jnp.bfloat16).at[slots].set(unit)
    core = lax.axis_index("shard") % 2
    outgoing_labels = jnp.full((SLOTS,), -1, jnp.int32).at[slots].set(cluster_ids)
    outgoing_labels = outgoing_labels.reshape(SHARDS, 1, CAP)
    blank = jnp.zeros_like(outgoing_labels)
    outgoing_labels = jnp.where(
        core == 0,
        jnp.concatenate([outgoing_labels, blank], axis=2),
        jnp.concatenate([blank, outgoing_labels], axis=2),
    )
    returned = exchange(outgoing.reshape(SHARDS, CAP, unit.shape[1]), outgoing_labels)
    totals = returned.reshape(SHARDS * LANES)[owner * LANES + core * CAP + ranks]
    return jnp.log(1.0 + totals)


def solution(mesh):
    in_specs = (P(("shard", "tile"), None), P(("shard", "tile")))
    out_specs = P(("shard", "tile"))
    return jax.shard_map(body, mesh=mesh, in_specs=in_specs, out_specs=out_specs, check_vma=False)
```

time: 300 us -> 150 us (0.50)
  Pallas kernels: 0 us -> 119 us
  waiting for transfers between devices: 93.9 us -> 0 us
  blocking collectives: 90.2 us -> 0 us
  matrix products: 53.3 us -> 0 us
  between operations: 14.2 us -> 0.1 us
  other arithmetic: 29.4 us -> 20.6 us
  starting transfers between devices: 3.85 us -> 0 us
  local copies, waits for them, and re-layouts: 13.8 us -> 10.5 us
    pallas_call x0 -> x1, Pallas kernels: none -> 119 us  [exchange(): pl.pallas_call(kernel, out_shape=jax.ShapeDtypeStruct((SHARDS, 1, LANES),...]
    all_gather x1 -> x0, waiting for transfers between devices: 88.2 us -> none  [body(): piece_rows = lax.all_gather(owned, 'tile', axis=0, tiled=True)]
    all_to_all x2 -> x0, blocking collectives: 66.5 us -> none  [the longest x1 48.2 us: body(): lax.all_to_all(outgoing.reshape(shards, capacity, unit.shape[1]), 'shard'...]
    dot_general x4 -> x0, matrix products: 53.3 us -> none  [step(): lax.dot_general(rows_block, right, (((1,), (1,)), ((), ())), preferred_el...]
    unnamed x1 -> x0, blocking collectives: 12 us -> none
    all_gather x1 -> x0, blocking collectives: 11.8 us -> none  [body(): piece_labels = lax.all_gather(owned_labels, 'tile', axis=0, tiled=True)]
    all_to_all x1 -> x0, waiting for transfers between devices: 5.76 us -> none  [body(): lax.all_to_all(outgoing_labels.reshape(shards, capacity), 'shard', split_...]
    add x5 -> x0, other arithmetic: 4.73 us -> none  [the longest x4 4.72 us: step(): return (column_total + jnp.sum(terms, axis=0), jnp.sum(terms, axis=1))]
  transfers between devices with their start and end apart: 2 -> 0, of which waited for: 2 -> 0; matrix products, arithmetic and copies ran while one was open for 2% -> 0% of each run, Pallas kernels for 0% -> 0%
where the time goes in v1:
time: 150 us
  Pallas kernels  119 us (79%)
  other arithmetic  20.6 us (14%)
  local copies, waits for them, and re-layouts  10.5 us (7%)
    pallas_call x1, Pallas kernels, exchange(): pl.pallas_call(kernel, out_shape=jax.ShapeDtypeStruct((SHARDS, 1, LANES),...  119 us
    another operation x2, other arithmetic  9.04 us
    scatter x1, other arithmetic, body(): jnp.zeros((SLOTS, unit.shape[1]), jnp.bfloat16).at[slots].set(unit)  7.72 us
    gather x1, local copies, waits for them, and re-layouts, body(): returned.reshape(SHARDS * LANES)[owner * LANES + core * CAP + ranks]  5.75 us
    scatter x1, local copies, waits for them, and re-layouts, body(): jnp.full((SLOTS,), -1, jnp.int32).at[slots].set(cluster_ids)  4.32 us

profile of v1, /device:TPU:1, one launch (start us, length us, event | category | flops | bytes accessed | tf_op | source)
XLA Modules:
  0.0 149.6 jit_solution(12474625210205480479)
XLA Ops:
  0.0 0.0 copy-start.1
  0.0 0.0 copy-start
  0.0 2.3 %multiply_reduce_fusion = f32[1024]{0:T(1024)S(1)} fusion(f32[1024,768]{1,0:T(8,128)} %param.2), kind=kLoop, calls=%fused_computation.4 | loop fusion | flops 1571840 | bytes 3149824 | tf_op jit(solution)/shard_map/reduce_sum | solution.py:25
  2.3 0.0 copy-done.1
  2.4 9.0 %reduce-window.6 = s32[32,8,128]{2,1,0:T(8,128)S(1)} reduce-window(s32[32,8,128]{2,1,0:T(8,128)S(1)} %fusion.5, s32[]{:T(128)} %constant.46.clone.1), window={size=1x1x128 pad=0_0x0_0x127_0}, to_apply=%region_0.0 | reduce-window | flops 4161536 | bytes 262148 | tf_op jit(solution)/shard_map/reduce-window
  11.4 0.1 slice.10
  11.5 0.1 copy.3
  11.7 0.1 copy.4
  11.7 0.1 add_add_fusion
  11.9 4.3 %scatter_custom_fusion.1 = s32[2048]{0:T(1024)S(1)} fusion(s32[1024]{0:T(1024)S(1)} %get-tuple-element.6, s32[1024]{0:T(1024)S(1)} %copy-done.1, s32[]{:T(128)} %constant.49.clone.1), kind=kCustom, calls=%fused_computation.25 | custom fusion | bytes 8196 | tf_op jit(solution)/shard_map/scatter | solution.py:357
  16.2 0.1 reshape.35
  16.3 0.7 broadcast_select_fusion.labels_ref
  17.0 0.0 copy-done
  17.0 7.7 %scatter_custom_fusion = bf16[2048,768]{1,0:T(8,128)(2,1)} fusion(s32[1024]{0:T(1024)S(1)} %get-tuple-element.6, f32[1024,768]{1,0:T(8,128)S(1)} %copy-done, f32[1024]{0:T(1024)S(1)} %add_rsqrt_fusion, bf16[]{:T(256)} %constant.24.clone.1), kind=kCustom, calls=%fused_computation.5 | custom fusion | flops 1572864 | bytes 6295554 | tf_op jit(solution)/shard_map/scatter | solution.py:355
  24.8 118.5 %shard_map.28 = f32[32,1,128]{2,1,0:T(1,128)} custom-call(bf16[32,64,768]{2,1,0:T(8,128)(2,1)} %bitcast.21, s32[32,1,128]{2,1,0:T(1,128)} %broadcast_select_fusion.labels_ref), custom_call_target="tpu_custom_call" | custom-call | tf_op jit(solution)/shard_map/pallas_call | solution.py:326
  143.3 5.8 %gather_fusion = f32[1024]{0:T(1024)S(1)} fusion(f32[4096]{0:T(1024)} %bitcast.20, s32[1024]{0:T(1024)S(1)} %get-tuple-element.5), kind=kCustom, calls=%fused_computation | custom fusion | bytes 12288 | tf_op jit(solution)/shard_map/gather | solution.py:366
  149.0 0.6 add_log_fusion
  (7 shorter events, 0.1 us)
Async XLA Ops:
  0.0 2.3 %copy-start.1 = (s32[1024]{0:T(1024)S(1)}, s32[1024]{0:T(1024)}, u32[]{:S(2)}) copy-start(s32[1024]{0:T(1024)} %param.3) | copy-start | bytes 12292
  0.0 17.0 %copy-start = (f32[1024,768]{1,0:T(8,128)S(1)}, f32[1024,768]{1,0:T(8,128)}, u32[]{:S(2)}) copy-start(f32[1024,768]{1,0:T(8,128)} %param.2) | copy-start | bytes 9437188

commit v2 on v1

--- a/solution.py
+++ b/solution.py
@@ -1,4 +1,3 @@
-import functools
 import math
 
 import jax
@@ -19,16 +18,12 @@
 epsilon = 1e-06
 EXP2_SCALE = sharpness / math.log(2.0)
 ROW_BLOCK = 512
-
-
-def unit_rows(embeddings):
-    energy = jnp.sum(embeddings * embeddings, axis=1, keepdims=True)
-    return (embeddings * lax.rsqrt(energy + epsilon)).astype(jnp.bfloat16)
+PLACE = 512
 
 
 def kernel(
-    rows_ref, labels_ref, out_ref,
-    rows, labels, row_labels, row_acc, col_f, col_h, col_in, totals, returned,
+    data_ref, ids_ref, out_ref,
+    unit, rows_ref, labels_ref, rows, labels, row_labels, row_acc, col_f, col_h, col_in, totals, returned,
     local_sem, a2a_send, a2a_recv, lab_send, lab_recv, z_send, z_recv,
     zlab_send, zlab_recv, col_send, col_recv, ret_send, ret_recv,
 ):
@@ -65,6 +60,56 @@
     def _(i):
         pl.semaphore_signal(barrier, inc=1, device_id=(s, (t + i) % 4), device_id_type=MESH)
 
+    ids = ids_ref[...]
+    owner = lax.shift_right_logical(ids, 4)
+    local = lax.bitwise_and(ids, KG - 1)
+    count = ids.shape[1]
+    is_owner = lax.broadcasted_iota(jnp.int32, (SHARDS, count), 0) == owner
+    onehot = jnp.where(is_owner, 1.0, 0.0)
+    onehot_bf16 = onehot.astype(jnp.bfloat16)
+    earlier = lax.broadcasted_iota(jnp.int32, (count, count), 0) < lax.broadcasted_iota(
+        jnp.int32, (count, count), 1
+    )
+    before = lax.dot_general(
+        onehot_bf16, jnp.where(earlier, 1.0, 0.0).astype(jnp.bfloat16), (((1,), (0,)), ((), ())),
+        preferred_element_type=jnp.float32,
+    )
+    ranks = jnp.sum(before * onehot, axis=0, keepdims=True).astype(jnp.int32)
+    slots = owner * CAP + ranks
+
+    @pl.loop(0, count // LANES)
+    def _(k):
+        here = pl.ds(pl.multiple_of(k * LANES, LANES), LANES)
+        block = data_ref[here, :]
+        energy = jnp.sum(block * block, axis=1, keepdims=True)
+        unit[here, :] = (block * lax.rsqrt(energy + epsilon)).astype(jnp.bfloat16)
+
+    tags = jnp.broadcast_to((local + 1).astype(jnp.float32), (8, count)).astype(jnp.bfloat16)
+    lane = lax.broadcasted_iota(jnp.int32, (1, LANES), 1)
+    in_half = (lane // CAP) == core
+
+    def place(k):
+        slot = lax.broadcasted_iota(jnp.int32, (PLACE, count), 0) + k * PLACE
+        chosen = jnp.where(slot == slots, 1.0, 0.0).astype(jnp.bfloat16)
+        rows_out = lax.dot_general(
+            chosen, unit[...], (((1,), (0,)), ((), ())), preferred_element_type=jnp.float32
+        ).astype(jnp.bfloat16)
+        for m in range(PLACE // CAP):
+            rows_ref[k * (PLACE // CAP) + m] = rows_out[m * CAP:(m + 1) * CAP]
+        tags_out = lax.dot_general(
+            tags, chosen, (((1,), (1,)), ((), ())), preferred_element_type=jnp.float32
+        )
+        for m in range(PLACE // LANES):
+            both = tags_out[:, m * LANES:(m + 1) * LANES]
+            swapped = pltpu.roll(both, CAP, 1)
+            for b in range(2):
+                value = jnp.where(core == b, both, swapped)[0:1]
+                labels_ref[k * (PLACE // CAP) + 2 * m + b] = jnp.where(in_half, value, 0.0)
+
+    @pl.loop(0, SLOTS // PLACE)
+    def _(k):
+        place(k)
+
     own_rows = pltpu.make_async_copy(rows_ref.at[s], chunk(0, s), local_sem.at[0])
     own_labels = pltpu.make_async_copy(labels_ref.at[s], labels.at[0, s], local_sem.at[1])
     own_rows.start()
@@ -180,7 +225,7 @@
     @pl.loop(0, SLOTS // LANES)
     def _(c):
         wide = jnp.broadcast_to(pair_labels(0, c), (LANES, LANES))
-        row_labels[pl.ds(pl.multiple_of(c * LANES, LANES), LANES), :] = wide.astype(jnp.float32).T
+        row_labels[pl.ds(pl.multiple_of(c * LANES, LANES), LANES), :] = wide.T
         row_acc[pl.ds(pl.multiple_of(c * LANES, LANES), LANES), :] = jnp.zeros((LANES, LANES), jnp.float32)
 
     @pl.loop(6, SHARDS)
@@ -203,7 +248,7 @@
             [rows[slot, pl.ds(pl.multiple_of(c * LANES, LANES), LANES), :] for c in chips], axis=0
         )
         column_labels = [
-            jnp.broadcast_to(pair_labels(slot, c), (8, LANES)).astype(jnp.float32)[0:1] for c in chips
+            pair_labels(slot, c) for c in chips
         ]
 
         def block(m, sums):
@@ -317,20 +362,35 @@
         ret_copy(i, p, p).wait_recv()
         ret_copy(i, peer(i, 1), s).wait_send()
 
-    out_ref[...] = returned[...]
-
-
-def exchange(outgoing, outgoing_labels):
-    width = outgoing.shape[-1]
+    back = returned[:, 0, :]
+    picked = None
+    for _ in range(3):
+        piece = back.astype(jnp.bfloat16)
+        back = back - piece.astype(jnp.float32)
+        part = lax.dot_general(
+            piece, onehot_bf16, (((0,), (0,)), ((), ())), preferred_element_type=jnp.float32
+        )
+        picked = part if picked is None else picked + part
+    at_rank = lax.broadcasted_iota(jnp.int32, (LANES, count), 0) == core * CAP + ranks
+    total = jnp.sum(jnp.where(at_rank, picked, 0.0), axis=0, keepdims=True)
+    out_ref[...] = jnp.log(1.0 + total)
+
+
+def body(embeddings, cluster_ids):
+    count, width = embeddings.shape
     dma = pltpu.SemaphoreType.DMA
-    return pl.pallas_call(
+    vmem = pl.BlockSpec(memory_space=pltpu.VMEM)
+    out = pl.pallas_call(
         kernel,
-        out_shape=jax.ShapeDtypeStruct((SHARDS, 1, LANES), jnp.float32),
-        in_specs=[pl.BlockSpec(memory_space=pl.ANY), pl.BlockSpec(memory_space=pltpu.VMEM)],
-        out_specs=pl.BlockSpec(memory_space=pltpu.VMEM),
+        out_shape=jax.ShapeDtypeStruct((1, count), jnp.float32),
+        in_specs=[vmem, vmem],
+        out_specs=vmem,
         scratch_shapes=[
+            pltpu.VMEM((count, width), jnp.bfloat16),
+            pltpu.VMEM((SHARDS, CAP, width), jnp.bfloat16),
+            pltpu.VMEM((SHARDS, 1, LANES), jnp.float32),
             pltpu.VMEM((3, SLOTS, width), jnp.bfloat16),
-            pltpu.VMEM((3, SHARDS, 1, LANES), jnp.int32),
+            pltpu.VMEM((3, SHARDS, 1, LANES), jnp.float32),
             pltpu.VMEM((SLOTS, LANES), jnp.float32),
             pltpu.VMEM((SLOTS, LANES), jnp.float32),
             pltpu.VMEM((SLOTS // LANES, 1, LANES), jnp.float32),
@@ -343,28 +403,8 @@
             dma((SHARDS,)), dma((SHARDS,)),
         ],
         compiler_params=pltpu.CompilerParams(collective_id=0, has_side_effects=True),
-    )(outgoing, outgoing_labels)
-
-
-def body(embeddings, cluster_ids):
-    unit = unit_rows(embeddings)
-    owner = cluster_ids // KG
-    onehot = (owner[:, None] == jnp.arange(SHARDS, dtype=jnp.int32)[None, :]).astype(jnp.int32)
-    ranks = jnp.sum((jnp.cumsum(onehot, axis=0) - 1) * onehot, axis=1)
-    slots = owner * CAP + ranks
-    outgoing = jnp.zeros((SLOTS, unit.shape[1]), jnp.bfloat16).at[slots].set(unit)
-    core = lax.axis_index("shard") % 2
-    outgoing_labels = jnp.full((SLOTS,), -1, jnp.int32).at[slots].set(cluster_ids)
-    outgoing_labels = outgoing_labels.reshape(SHARDS, 1, CAP)
-    blank = jnp.zeros_like(outgoing_labels)
-    outgoing_labels = jnp.where(
-        core == 0,
-        jnp.concatenate([outgoing_labels, blank], axis=2),
-        jnp.concatenate([blank, outgoing_labels], axis=2),
-    )
-    returned = exchange(outgoing.reshape(SHARDS, CAP, unit.shape[1]), outgoing_labels)
-    totals = returned.reshape(SHARDS * LANES)[owner * LANES + core * CAP + ranks]
-    return jnp.log(1.0 + totals)
+    )(embeddings, cluster_ids.reshape(1, count))
+    return out.reshape(count)
 
 
 def solution(mesh):

time: 150 us -> 126 us (0.84)
  other arithmetic: 20.6 us -> 0 us
  local copies, waits for them, and re-layouts: 10.5 us -> 1.28 us
  Pallas kernels: 119 us -> 124 us
    another operation x2 -> x0, other arithmetic: 9.04 us -> none
    scatter x1 -> x0, other arithmetic: 7.72 us -> none  [body(): jnp.zeros((SLOTS, unit.shape[1]), jnp.bfloat16).at[slots].set(unit)]
    pallas_call x1, Pallas kernels: 119 us -> 124 us  [body(): pl.pallas_call(kernel, out_shape=jax.ShapeDtypeStruct((1, count), jnp.flo...]
    gather x1 -> x0, local copies, waits for them, and re-layouts: 5.75 us -> none  [body(): returned.reshape(SHARDS * LANES)[owner * LANES + core * CAP + ranks]]
    scatter x1 -> x0, local copies, waits for them, and re-layouts: 4.32 us -> none  [body(): jnp.full((SLOTS,), -1, jnp.int32).at[slots].set(cluster_ids)]
    reduce_sum x2 -> x0, other arithmetic: 2.35 us -> none  [the longest x1 2.31 us: unit_rows(): energy = jnp.sum(embeddings * embeddings, axis=1, keepdims=True)]
where the time goes in v2:
time: 126 us
  Pallas kernels  124 us (98%)
  local copies, waits for them, and re-layouts  1.28 us (1%)
    pallas_call x1, Pallas kernels, body(): pl.pallas_call(kernel, out_shape=jax.ShapeDtypeStruct((1, count), jnp.flo...  124 us

profile of v2, /device:TPU:1, one launch (start us, length us, event | category | flops | bytes accessed | tf_op | source)
XLA Modules:
  0.0 125.7 jit_solution(6982751809143111148)
XLA Ops:
  0.0 124.4 %shard_map.28 = f32[1,1024]{1,0:T(1,128)} custom-call(f32[1024,768]{1,0:T(8,128)} %data_ref.1, s32[1,1024]{1,0:T(1,128)} %bitcast.3), custom_call_target="tpu_custom_call" | custom-call | tf_op jit(solution)/shard_map/pallas_call | solution.py:383
  124.4 1.3 %copy.4 = f32[1024]{0:T(1024)} copy(f32[1024]{0:T(1024)} %bitcast.2) | data formatting | bytes 8192
